TPU v7x, 32 devices: a whole 2x2x4 slice. The times are simulated.
32 devices in a mesh: feat: 8 (over z, core), col: 4 (over y, x).
Axes of the slice: x: 2, y: 2, z: 4, core: 2. Of those that a mesh axis runs over, the one named last changes fastest.
Arguments:
- self_feats: bfloat16 [4096, 128], P(('feat', 'col')), may hold values from -6 to 6
- neighbour_feats: bfloat16 [128, 16384], P('feat', 'col'), may hold values from -6 to 6
- tiles: bfloat16 [1024, 128, 128], P('col'), may hold values from 0 to 1, as said below
- tile_rows: int32 [1024], P('col'), may hold values from 0 to 31, as said below
- tile_cols: int32 [1024], P('col'), may hold values from 0 to 31
- tile_count: int32 [4], P('col'), may hold values from 1 to 256, 768 in all
- owner_order: int32 [32], replicated, may hold values from 0 to 31, as said below
- degree: int32 [4096], P(('feat', 'col')), may hold values from 64 to 192
- w_self: bfloat16 [128, 256], replicated, may hold values from -0.5 to 0.5
- w_neigh: bfloat16 [128, 256], replicated, may hold values from -0.5 to 0.5
- bias: float32 [256], replicated, may hold values from -3 to 3
- upstream: bfloat16 [4096, 256], P(('feat', 'col')), may hold values from -6 to 6
Outputs:
- hidden_out: bfloat16 [4096, 256], P(('feat', 'col'))
- neigh_grad: bfloat16 [128, 16384], P('feat', 'col')
Inputs may be any that keep to these rules, and one draw needn't show every extreme that they name: `tiles`: every entry is 0 or 1. `tile_count`: slots at or after a group's count are ignored; some group has all 256 slots live. `owner_order`: a permutation of the row blocks. `tile_rows`: in every column group, slot s has a row block whose owner position p satisfies (p) % 4 == s % 4.
All inputs are finite; a program needn't handle non-finite values.
Results may differ from a plain program's by a relative error of at most 0.0065.
Values may be sent and summed in bfloat16 or wider, within the bound.
No kernel may reach another device: no remote copies, remote signals or barrier semaphores. Data moves between devices by JAX's collectives and lax.ppermute only.
A program may use at most 64 MiB of HBM per device.

v0:
```python
import jax
import jax.numpy as jnp
from jax import lax
from jax.sharding import PartitionSpec as P


def local(
    self_feats,
    neighbour_feats,
    tiles,
    tile_rows,
    tile_cols,
    tile_count,
    owner_order,
    degree,
    w_self,
    w_neigh,
    bias,
    upstream,
):
    nfeat = lax.axis_size("feat")
    ncol = lax.axis_size("col")
    slots, tile_size, _ = tiles.shape
    slice_width = neighbour_feats.shape[0]
    col_blocks = neighbour_feats.shape[1] // tile_size
    row_blocks = self_feats.shape[0] // tile_size
    blocks_total = owner_order.shape[0]
    places = (
        jnp.zeros((blocks_total,), jnp.int32)
        .at[owner_order]
        .set(jnp.arange(blocks_total, dtype=jnp.int32))
    )
    target = places[tile_rows]
    live = (jnp.arange(slots, dtype=jnp.int32) < tile_count[0]).astype(jnp.float32)
    blocked = neighbour_feats.reshape(slice_width, col_blocks, tile_size).transpose(1, 0, 2)
    picked = blocked[tile_cols]
    products = (
        jnp.einsum("nfk,nrk->nfr", picked, tiles, preferred_element_type=jnp.float32)
        * live[:, None, None]
    )
    partial_value = (
        jnp.zeros((blocks_total, slice_width, tile_size), jnp.float32).at[target].add(products)
    )
    grid = partial_value.reshape(nfeat, ncol, row_blocks, slice_width, tile_size)
    total = lax.psum(grid, "col")
    mine = lax.dynamic_slice_in_dim(total, lax.axis_index("col"), 1, 1)
    owned = lax.all_to_all(mine, "feat", split_axis=0, concat_axis=1, tiled=True)
    summed = owned.reshape(nfeat, row_blocks, slice_width, tile_size).transpose(1, 3, 0, 2)
    summed = summed.reshape(row_blocks * tile_size, nfeat * slice_width)
    scale = lax.rsqrt(degree.astype(jnp.float32))[:, None]
    aggregate = (summed * scale).astype(jnp.bfloat16)
    pre = jnp.dot(self_feats, w_self, preferred_element_type=jnp.float32)
    pre = pre + jnp.dot(aggregate, w_neigh, preferred_element_type=jnp.float32) + bias
    gate = jax.nn.sigmoid(pre)
    hidden_out = (pre * gate).astype(jnp.bfloat16)
    slope = gate * (1.0 + pre * (1.0 - gate))
    dpre = (upstream.astype(jnp.float32) * slope).astype(jnp.bfloat16)
    dagg = lax.dot_general(
        dpre, w_neigh, (((1,), (1,)), ((), ())), preferred_element_type=jnp.float32
    )
    back = (dagg * scale).astype(jnp.bfloat16)
    arranged = back.reshape(row_blocks, tile_size, nfeat, slice_width).transpose(2, 0, 3, 1)
    arranged = arranged.reshape(nfeat, 1, row_blocks, slice_width, tile_size)
    regrouped = lax.all_to_all(arranged, "feat", split_axis=0, concat_axis=0, tiled=True)
    everything = lax.all_gather(regrouped, "col", axis=1, tiled=True)
    row_grads = everything.reshape(blocks_total, slice_width, tile_size)
    taken = row_grads[target]
    pieces = (
        jnp.einsum("nfr,nrk->nfk", taken, tiles, preferred_element_type=jnp.float32)
        * live[:, None, None]
    )
    onehot_cols = (tile_cols[:, None] == jnp.arange(col_blocks, dtype=jnp.int32)[None, :]).astype(
        jnp.float32
    )
    col_total = jnp.einsum("nc,nfk->fck", onehot_cols, pieces, precision=lax.Precision.HIGHEST)
    neigh_grad = col_total.reshape(slice_width, col_blocks * tile_size).astype(jnp.bfloat16)
    return (hidden_out, neigh_grad)


def solution(mesh):
    in_specs = (
        P(("feat", "col"), None),
        P("feat", "col"),
        P("col", None, None),
        P("col"),
        P("col"),
        P("col"),
        P(),
        P(("feat", "col")),
        P(),
        P(),
        P(),
        P(("feat", "col"), None),
    )
    out_specs = (P(("feat", "col"), None), P("feat", "col"))
    return jax.shard_map(local, mesh=mesh, in_specs=in_specs, out_specs=out_specs, check_vma=False)
```

profile of v0, /device:TPU:0, one launch (start us, length us, event | category | flops | bytes accessed | tf_op | source)
XLA Modules:
  0.0 141.6 jit_solution(16048866213782390295)
XLA Ops:
  7.2 0.0 copy-start
  7.2 0.0 all-reduce.2.cloned.1.call-start
  7.2 0.7 compare_select_fusion.3
  7.9 0.7 scatter_custom_fusion
  8.6 0.7 fusion.14
  9.3 0.7 fusion.15
  10.0 20.7 %compare_select_fusion.4 = s32[256]{0:T(256)S(1)} fusion(s32[256]{0:T(256)} %param.15, s32[]{:T(128)} %bitcast, s32[]{:T(128)} %bitcast.1, s32[]{:T(128)} %bitcast.2, s32[]{:T(128)} %bitcast.3, s32[]{:T(128)} %bitcast.4, s32[]{:T(128)} %bitcast.5, s32[]{:T(128)} %bitcast.6, s32[]{:T(128)} %bitcast.7, s32[]{:T(128)} %bitcast.8, s32[]{:T(128)} %bitcast.9, ...), kind=kLoop, calls=%fused_computation.30 | loop fusion | flops 16640 | bytes 2176 | tf_op jit(solution)/shard_map/gather | solution.py:33
  31.4 0.0 copy-done
  31.5 0.7 compare_select_fusion.1
  32.2 0.8 gather_fusion
  33.0 6.8 %convolution_multiply_fusion.1 = f32[256,16,128]{2,1,0:T(8,128)S(1)} fusion(bf16[256,16,128]{2,1,0:T(8,128)(2,1)S(1)} %gather_fusion, bf16[256,128,128]{2,1,0:T(8,128)(2,1)} %param.14, f32[256]{0:T(256)S(1)} %compare_convert_fusion), kind=kOutput, calls=%fused_computation.7 | convolution fusion | flops 134742016 | bytes 11535360 | tf_op jit(solution)/shard_map/nfk,nrk->nfr/dot_general | solution.py:38
  39.9 0.0 copy-start.2
  39.9 0.0 copy-start.3
  39.9 0.0 copy-start.8
  39.9 0.0 copy-start.5
  39.9 0.0 copy-start.7
  39.9 0.0 copy-start.6
  39.9 9.0 %scatter_fusion = f32[32,16,128]{2,1,0:T(8,128)S(1)} fusion(f32[32,16,128]{2,1,0:T(8,128)S(1)} %broadcast_in_dim.8, s32[256]{0:T(256)S(1)} %bitcast.83, f32[256,16,128]{2,1,0:T(8,128)S(1)} %convolution_multiply_fusion.1), kind=kCustom, calls=%fused_computation.3 | custom fusion | flops 524288 | bytes 6292480 | tf_op jit(solution)/shard_map/scatter-add | solution.py:42
  48.9 0.0 copy-start.1
  48.9 0.7 copy-done.1
  49.6 0.0 all-reduce.2.cloned.1.call-update
  49.6 0.0 copy-done.2
  49.6 0.0 copy-done.3
  49.6 0.1 fusion.16
  49.8 45.6 %all-reduce.2.cloned.1.call-done = f32[8,4,1,16,128]{4,3,1,0,2:T(8,128)} async-done(((f32[8,4,1,16,128]{4,3,1,0,2:T(8,128)}), f32[8,4,1,16,128]{4,3,1,0,2:T(8,128)}) %all-reduce.2.cloned.1.call-update) | async-done | bytes 262160 | tf_op jit(solution)/shard_map/psum | solution.py:45
  95.4 1.5 %dynamic-slice_bitcast_fusion = f32[8,1,1,16,128]{4,3,1,2,0:T(8,128)} fusion(f32[8,4,1,16,128]{4,3,1,0,2:T(8,128)} %all-reduce.2.cloned.1.call-done, s32[]{:T(128)S(6)} %select_n.27), kind=kLoop, calls=%fused_computation.20 | loop fusion | bytes 131076 | tf_op jit(solution)/shard_map/dynamic_slice | solution.py:46
  96.9 4.6 %all-to-all-start = ((f32[8,1,1,16,128]{4,3,1,2,0:T(8,128)}), f32[8,1,1,16,128]{4,3,1,2,0:T(8,128)S(1)}, u32[]{:S(2)}, u32[]{:S(2)}) async-start(f32[8,1,1,16,128]{4,3,1,2,0:T(8,128)} %dynamic-slice_bitcast_fusion), calls=%async_computation | async-start | bytes 131072 | tf_op jit(solution)/shard_map/all_to_all | solution.py:47
  101.5 0.0 copy-done.8
  101.5 5.9 %all-to-all-done = f32[8,1,1,16,128]{4,3,1,2,0:T(8,128)S(1)} async-done(((f32[8,1,1,16,128]{4,3,1,2,0:T(8,128)}), f32[8,1,1,16,128]{4,3,1,2,0:T(8,128)S(1)}, u32[]{:S(2)}, u32[]{:S(2)}) %all-to-all-start) | async-done | bytes 65568 | tf_op jit(solution)/shard_map/all_to_all | solution.py:47
  107.4 0.0 copy-done.5
  107.4 0.0 copy-done.7
  107.4 0.9 multiply_convert_fusion.1
  108.3 0.0 copy-done.6
  108.3 0.8 fusion.6
  109.1 3.3 %all-to-all-start.1 = ((bf16[8,1,1,16,128]{4,3,1,2,0:T(8,128)(2,1)}), bf16[8,1,1,16,128]{4,3,1,2,0:T(8,128)(2,1)S(1)}, u32[]{:S(2)}, u32[]{:S(2)}) async-start(bf16[8,1,1,16,128]{4,3,1,2,0:T(8,128)(2,1)} %bitcast.43), calls=%async_computation.1 | async-start | bytes 65536 | tf_op jit(solution)/shard_map/all_to_all | solution.py:64
  112.5 5.7 %all-to-all-done.1 = bf16[8,1,1,16,128]{4,3,1,2,0:T(8,128)(2,1)S(1)} async-done(((bf16[8,1,1,16,128]{4,3,1,2,0:T(8,128)(2,1)}), bf16[8,1,1,16,128]{4,3,1,2,0:T(8,128)(2,1)S(1)}, u32[]{:S(2)}, u32[]{:S(2)}) %all-to-all-start.1) | async-done | bytes 32800 | tf_op jit(solution)/shard_map/all_to_all | solution.py:64
  118.1 8.9 %all_gather.3 = bf16[8,4,1,16,128]{4,3,1,0,2:T(8,128)(2,1)S(1)} all-gather(bf16[8,1,1,16,128]{4,3,1,0,2:T(8,128)(2,1)S(1)} %bitcast.81), channel_id=1, replica_groups=mesh['feat'=8,'col'=4] {'col'}, dimensions={1}, use_global_device_ids=true | all-gather | bytes 163840 | tf_op jit(solution)/shard_map/all_gather | solution.py:65
  127.1 0.8 gather_fusion.1
  127.9 0.0 copy-start.4
  127.9 4.7 %convolution_multiply_fusion = f32[256,16,128]{2,1,0:T(8,128)S(1)} fusion(bf16[256,16,128]{2,1,0:T(8,128)(2,1)S(1)} %gather_fusion.1, bf16[256,128,128]{2,1,0:T(8,128)(2,1)} %param.14, f32[256]{0:T(256)S(1)} %compare_convert_fusion), kind=kOutput, calls=%fused_computation.6 | convolution fusion | flops 134742016 | bytes 11535360 | tf_op jit(solution)/shard_map/nfr,nrk->nfk/dot_general | solution.py:69
  132.6 0.0 copy-done.4
  132.6 1.4 fusion.2
  134.0 0.7 copy.30
  (9 shorter events, 0.1 us)
Async XLA Ops:
  7.2 24.3 %copy-start = (bf16[16,4096]{1,0:T(8,128)(2,1)S(1)}, bf16[16,4096]{1,0:T(8,128)(2,1)}, u32[]{:S(2)}) copy-start(bf16[16,4096]{1,0:T(8,128)(2,1)} %param.13) | copy-start | bytes 393220
  7.2 88.2 %all-reduce.2.cloned.1.call-start = ((), (), s32[]{:S(2)}) async-start(), calls=%async_computation.2 | async-start | bytes 524288 | tf_op jit(solution)/shard_map/psum | solution.py:45
  39.9 9.8 %copy-start.2 = (bf16[128,256]{1,0:T(8,128)(2,1)S(1)}, bf16[128,256]{1,0:T(8,128)(2,1)}, u32[]{:S(2)}) copy-start(bf16[128,256]{1,0:T(8,128)(2,1)} %param.20) | copy-start | bytes 196612
  39.9 9.8 %copy-start.3 = (bf16[128,128]{1,0:T(8,128)(2,1)S(1)}, bf16[128,128]{1,0:T(8,128)(2,1)}, u32[]{:S(2)}) copy-start(bf16[128,128]{1,0:T(8,128)(2,1)} %param.12) | copy-start | bytes 98308
  39.9 61.6 %copy-start.8 = (s32[128]{0:T(128)S(1)}, s32[128]{0:T(128)}, u32[]{:S(2)}) copy-start(s32[128]{0:T(128)} %param.19) | copy-start | bytes 1540
  39.9 67.5 %copy-start.5 = (bf16[128,256]{1,0:T(8,128)(2,1)S(1)}, bf16[128,256]{1,0:T(8,128)(2,1)}, u32[]{:S(2)}) copy-start(bf16[128,256]{1,0:T(8,128)(2,1)} %param.21) | copy-start | bytes 196612
  39.9 67.5 %copy-start.7 = (f32[256]{0:T(256)S(1)}, f32[256]{0:T(256)}, u32[]{:S(2)}) copy-start(f32[256]{0:T(256)} %param.22) | copy-start | bytes 3076
  39.9 68.4 %copy-start.6 = (bf16[128,256]{1,0:T(8,128)(2,1)S(1)}, bf16[128,256]{1,0:T(8,128)(2,1)}, u32[]{:S(2)}) copy-start(bf16[128,256]{1,0:T(8,128)(2,1)} %param.23) | copy-start | bytes 196612
  48.9 0.7 copy-start.1
  96.9 10.5 %all-to-all-start = ((f32[8,1,1,16,128]{4,3,1,2,0:T(8,128)}), f32[8,1,1,16,128]{4,3,1,2,0:T(8,128)S(1)}, u32[]{:S(2)}, u32[]{:S(2)}) async-start(f32[8,1,1,16,128]{4,3,1,2,0:T(8,128)} %dynamic-slice_bitcast_fusion), calls=%async_computation | async-start | bytes 131072 | tf_op jit(solution)/shard_map/all_to_all | solution.py:47
  109.1 9.0 %all-to-all-start.1 = ((bf16[8,1,1,16,128]{4,3,1,2,0:T(8,128)(2,1)}), bf16[8,1,1,16,128]{4,3,1,2,0:T(8,128)(2,1)S(1)}, u32[]{:S(2)}, u32[]{:S(2)}) async-start(bf16[8,1,1,16,128]{4,3,1,2,0:T(8,128)(2,1)} %bitcast.43), calls=%async_computation.1 | async-start | bytes 65536 | tf_op jit(solution)/shard_map/all_to_all | solution.py:64
  127.9 4.7 %copy-start.4 = (s32[256]{0:T(256)S(1)}, s32[256]{0:T(256)}, u32[]{:S(2)}) copy-start(s32[256]{0:T(256)} %param.16) | copy-start | bytes 3076
Sparse Core Ops, SparseCore 0:
  49.7 45.6 all-reduce.1
where the time goes:
time: 142 us
  waiting for transfers between devices  57.2 us (40%)
  other arithmetic  31.1 us (22%)
  between operations  14.9 us (10%)
  matrix products  14.7 us (10%)
  blocking collectives  8.92 us (6%)
  starting transfers between devices  7.98 us (6%)
  local copies, waits for them, and re-layouts  6.79 us (5%)
    psum x1, waiting for transfers between devices, local(): total = lax.psum(grid, 'col')  45.6 us
    gather x1, other arithmetic, local(): target = places[tile_rows]  20.7 us
    scatter-add x1, other arithmetic, local(): jnp.zeros((blocks_total, slice_width, tile_size), jnp.float32).at[target]  8.97 us
    all_gather x1, blocking collectives, local(): everything = lax.all_gather(regrouped, 'col', axis=1, tiled=True)  8.92 us
    dot_general x1, matrix products, local(): jnp.einsum('nfk,nrk->nfr', picked, tiles, preferred_element_type=jnp.floa...  6.77 us
    all_to_all x1, waiting for transfers between devices, local(): lax.all_to_all(mine, 'feat', split_axis=0, concat_axis=1, tiled=True)  5.9 us
    all_to_all x1, waiting for transfers between devices, local(): lax.all_to_all(arranged, 'feat', split_axis=0, concat_axis=0, tiled=True)  5.66 us
    dot_general x1, matrix products, local(): jnp.einsum('nfr,nrk->nfk', taken, tiles, preferred_element_type=jnp.float32)  4.68 us
  transfers between devices with their start and end apart: 3, of which 3 were waited for; matrix products, arithmetic and copies ran while one was open for 0% of the time, Pallas kernels for 0%

commit v1 on v0

--- a/solution.py
+++ b/solution.py
@@ -62,7 +62,12 @@
     arranged = back.reshape(row_blocks, tile_size, nfeat, slice_width).transpose(2, 0, 3, 1)
     arranged = arranged.reshape(nfeat, 1, row_blocks, slice_width, tile_size)
     regrouped = lax.all_to_all(arranged, "feat", split_axis=0, concat_axis=0, tiled=True)
-    everything = lax.all_gather(regrouped, "col", axis=1, tiled=True)
+    ring = [regrouped]
+    for hop in range(3):
+        ring.append(lax.ppermute(ring[-1], "col", [(dev, (dev + 1) % 4) for dev in range(4)]))
+    everything = jnp.roll(
+        jnp.concatenate(ring[::-1], axis=1), (lax.axis_index("col") + 1) * ring[0].shape[1], axis=1
+    )
     row_grads = everything.reshape(blocks_total, slice_width, tile_size)
     taken = row_grads[target]
     pieces = (

time: 142 us -> 146 us (1.028)
  waiting for transfers between devices: 57.2 us -> 63.9 us
    ppermute x0 -> x3, waiting for transfers between devices: none -> 12.4 us  [local(): lax.ppermute(ring[-1], 'col', [(dev, (dev + 1) % 4) for dev in range(4)])]
    all_gather x1 -> x0, blocking collectives: 8.92 us -> none  [local(): everything = lax.all_gather(regrouped, 'col', axis=1, tiled=True)]
    all_to_all x0 -> x1, blocking collectives: none -> 8.12 us  [local(): lax.all_to_all(arranged, 'feat', split_axis=0, concat_axis=0, tiled=True)]
    all_to_all x1 -> x0, waiting for transfers between devices: 5.66 us -> none  [local(): lax.all_to_all(arranged, 'feat', split_axis=0, concat_axis=0, tiled=True)]
    all_to_all x1 -> x0, starting transfers between devices: 3.34 us -> none  [local(): lax.all_to_all(arranged, 'feat', split_axis=0, concat_axis=0, tiled=True)]
    ppermute x0 -> x3, starting transfers between devices: none -> 2.02 us  [local(): lax.ppermute(ring[-1], 'col', [(dev, (dev + 1) % 4) for dev in range(4)])]
  transfers between devices with their start and end apart: 3 -> 5, of which waited for: 3 -> 5; matrix products, arithmetic and copies ran while one was open for 0% -> 0% of each run, Pallas kernels for 0% -> 0%
where the time goes in v1:
time: 146 us
  waiting for transfers between devices  63.9 us (44%)
  other arithmetic  31.1 us (21%)
  between operations  15 us (10%)
  matrix products  14 us (10%)
  blocking collectives  8.12 us (6%)
  local copies, waits for them, and re-layouts  6.9 us (5%)
  starting transfers between devices  6.66 us (5%)
    psum x1, waiting for transfers between devices, local(): total = lax.psum(grid, 'col')  45.6 us
    gather x1, other arithmetic, local(): target = places[tile_rows]  20.8 us
    ppermute x3, waiting for transfers between devices, local(): lax.ppermute(ring[-1], 'col', [(dev, (dev + 1) % 4) for dev in range(4)])  12.4 us
    scatter-add x1, other arithmetic, local(): jnp.zeros((blocks_total, slice_width, tile_size), jnp.float32).at[target]  8.97 us
    all_to_all x1, blocking collectives, local(): lax.all_to_all(arranged, 'feat', split_axis=0, concat_axis=0, tiled=True)  8.12 us
    dot_general x1, matrix products, local(): jnp.einsum('nfk,nrk->nfr', picked, tiles, preferred_element_type=jnp.floa...  6.77 us
    all_to_all x1, waiting for transfers between devices, local(): lax.all_to_all(mine, 'feat', split_axis=0, concat_axis=1, tiled=True)  5.9 us
    dot_general x1, matrix products, local(): jnp.einsum('nfr,nrk->nfk', taken, tiles, preferred_element_type=jnp.float32)  4.68 us
  transfers between devices with their start and end apart: 5, of which 5 were waited for; matrix products, arithmetic and copies ran while one was open for 0% of the time, Pallas kernels for 0%

profile of v1, /device:TPU:0, one launch (start us, length us, event | category | flops | bytes accessed | tf_op | source)
XLA Modules:
  0.0 145.7 jit_solution(14342107557298035952)
XLA Ops:
  7.2 0.0 copy-start
  7.2 0.0 all-reduce.2.cloned.1.call-start
  7.2 0.7 compare_select_fusion.3
  7.9 0.7 scatter_custom_fusion
  8.6 0.7 fusion.14
  9.3 0.7 fusion.15
  10.0 20.8 %compare_select_fusion.4 = s32[256]{0:T(256)S(1)} fusion(s32[256]{0:T(256)} %param.15, s32[]{:T(128)} %bitcast, s32[]{:T(128)} %bitcast.1, s32[]{:T(128)} %bitcast.2, s32[]{:T(128)} %bitcast.3, s32[]{:T(128)} %bitcast.4, s32[]{:T(128)} %bitcast.5, s32[]{:T(128)} %bitcast.6, s32[]{:T(128)} %bitcast.7, s32[]{:T(128)} %bitcast.8, s32[]{:T(128)} %bitcast.9, ...), kind=kLoop, calls=%fused_computation.38 | loop fusion | flops 16640 | bytes 2176 | tf_op jit(solution)/shard_map/gather | solution.py:33
  31.5 0.0 copy-done
  31.5 0.7 compare_select_fusion.1
  32.2 0.8 gather_fusion
  33.1 6.8 %convolution_multiply_fusion.1 = f32[256,16,128]{2,1,0:T(8,128)S(1)} fusion(bf16[256,16,128]{2,1,0:T(8,128)(2,1)S(1)} %gather_fusion, bf16[256,128,128]{2,1,0:T(8,128)(2,1)} %param.14, f32[256]{0:T(256)S(1)} %compare_convert_fusion), kind=kOutput, calls=%fused_computation.7 | convolution fusion | flops 134742016 | bytes 11535360 | tf_op jit(solution)/shard_map/nfk,nrk->nfr/dot_general | solution.py:38
  39.9 0.0 copy-start.2
  39.9 0.0 copy-start.3
  39.9 0.0 copy-start.8
  39.9 0.0 copy-start.5
  39.9 0.0 copy-start.7
  39.9 0.0 copy-start.6
  39.9 9.0 %scatter_fusion = f32[32,16,128]{2,1,0:T(8,128)S(1)} fusion(f32[32,16,128]{2,1,0:T(8,128)S(1)} %broadcast_in_dim.8, s32[256]{0:T(256)S(1)} %bitcast.88, f32[256,16,128]{2,1,0:T(8,128)S(1)} %convolution_multiply_fusion.1), kind=kCustom, calls=%fused_computation.3 | custom fusion | flops 524288 | bytes 6292480 | tf_op jit(solution)/shard_map/scatter-add | solution.py:42
  48.9 0.0 copy-start.1
  48.9 0.7 copy-done.1
  49.6 0.0 all-reduce.2.cloned.1.call-update
  49.7 0.0 copy-done.2
  49.7 0.0 copy-done.3
  49.7 0.1 fusion.16
  49.8 45.6 %all-reduce.2.cloned.1.call-done = f32[8,4,1,16,128]{4,3,1,0,2:T(8,128)} async-done(((f32[8,4,1,16,128]{4,3,1,0,2:T(8,128)}), f32[8,4,1,16,128]{4,3,1,0,2:T(8,128)}) %all-reduce.2.cloned.1.call-update) | async-done | bytes 262160 | tf_op jit(solution)/shard_map/psum | solution.py:45
  95.5 1.5 %dynamic-slice_bitcast_fusion = f32[8,1,1,16,128]{4,3,1,2,0:T(8,128)} fusion(f32[8,4,1,16,128]{4,3,1,0,2:T(8,128)} %all-reduce.2.cloned.1.call-done, s32[]{:T(128)S(6)} %select_n.40), kind=kLoop, calls=%fused_computation.20 | loop fusion | bytes 131076 | tf_op jit(solution)/shard_map/dynamic_slice | solution.py:46
  96.9 4.6 %all-to-all-start = ((f32[8,1,1,16,128]{4,3,1,2,0:T(8,128)}), f32[8,1,1,16,128]{4,3,1,2,0:T(8,128)S(1)}, u32[]{:S(2)}, u32[]{:S(2)}) async-start(f32[8,1,1,16,128]{4,3,1,2,0:T(8,128)} %dynamic-slice_bitcast_fusion), calls=%async_computation | async-start | bytes 131072 | tf_op jit(solution)/shard_map/all_to_all | solution.py:47
  101.5 0.0 copy-done.8
  101.6 5.9 %all-to-all-done = f32[8,1,1,16,128]{4,3,1,2,0:T(8,128)S(1)} async-done(((f32[8,1,1,16,128]{4,3,1,2,0:T(8,128)}), f32[8,1,1,16,128]{4,3,1,2,0:T(8,128)S(1)}, u32[]{:S(2)}, u32[]{:S(2)}) %all-to-all-start) | async-done | bytes 65568 | tf_op jit(solution)/shard_map/all_to_all | solution.py:47
  107.5 0.0 copy-done.5
  107.5 0.0 copy-done.7
  107.5 0.9 multiply_convert_fusion.1
  108.3 0.0 copy-done.6
  108.3 0.2 fusion.6
  108.5 8.1 %all_to_all.14 = bf16[8,1,1,16,128]{4,3,1,2,0:T(8,128)(2,1)S(1)} all-to-all(bf16[8,1,1,16,128]{4,3,1,2,0:T(8,128)(2,1)S(1)} %bitcast.87), channel_id=1, replica_groups=mesh['feat'=8,'col'=4] {'feat'}, dimensions={0} | all-to-all | bytes 65536 | tf_op jit(solution)/shard_map/all_to_all | solution.py:64
  116.7 1.5 collective-permute-start
  118.1 3.4 %collective-permute-done = bf16[8,1,1,16,128]{4,3,1,0,2:T(8,128)(2,1)S(1)} collective-permute-done((bf16[8,1,1,16,128]{4,3,1,0,2:T(8,128)(2,1)S(1)}, bf16[8,1,1,16,128]{4,3,1,0,2:T(8,128)(2,1)S(1)}, u32[]{:S(2)}, u32[]{:S(2)}) %collective-permute-start) | collective-permute-done | bytes 32800 | tf_op jit(solution)/shard_map/ppermute | solution.py:67
  121.5 0.6 collective-permute-start.1
  122.0 4.3 %collective-permute-done.1 = bf16[8,1,1,16,128]{4,3,1,0,2:T(8,128)(2,1)S(1)} collective-permute-done((bf16[8,1,1,16,128]{4,3,1,0,2:T(8,128)(2,1)S(1)}, bf16[8,1,1,16,128]{4,3,1,0,2:T(8,128)(2,1)S(1)}, u32[]{:S(2)}, u32[]{:S(2)}) %collective-permute-start.1) | collective-permute-done | bytes 32800 | tf_op jit(solution)/shard_map/ppermute | solution.py:67
  126.3 0.0 collective-permute-start.2
  126.3 4.8 %collective-permute-done.2 = bf16[8,1,1,16,128]{4,3,1,0,2:T(8,128)(2,1)S(1)} collective-permute-done((bf16[8,1,1,16,128]{4,3,1,0,2:T(8,128)(2,1)S(1)}, bf16[8,1,1,16,128]{4,3,1,0,2:T(8,128)(2,1)S(1)}, u32[]{:S(2)}, u32[]{:S(2)}) %collective-permute-start.2) | collective-permute-done | bytes 32800 | tf_op jit(solution)/shard_map/ppermute | solution.py:67
  131.2 0.9 gather_fusion.1
  132.1 0.0 copy-start.4
  132.1 4.7 %convolution_multiply_fusion = f32[256,16,128]{2,1,0:T(8,128)S(1)} fusion(bf16[256,16,128]{2,1,0:T(8,128)(2,1)S(1)} %gather_fusion.1, bf16[256,128,128]{2,1,0:T(8,128)(2,1)} %param.14, f32[256]{0:T(256)S(1)} %compare_convert_fusion), kind=kOutput, calls=%fused_computation.6 | convolution fusion | flops 134742016 | bytes 11535360 | tf_op jit(solution)/shard_map/nfr,nrk->nfk/dot_general | solution.py:74
  136.8 0.0 copy-done.4
  136.8 1.4 fusion.2
  138.2 0.7 copy.32
  (18 shorter events, 0.2 us)
Async XLA Ops:
  7.2 24.3 %copy-start = (bf16[16,4096]{1,0:T(8,128)(2,1)S(1)}, bf16[16,4096]{1,0:T(8,128)(2,1)}, u32[]{:S(2)}) copy-start(bf16[16,4096]{1,0:T(8,128)(2,1)} %param.13) | copy-start | bytes 393220
  7.2 88.3 %all-reduce.2.cloned.1.call-start = ((), (), s32[]{:S(2)}) async-start(), calls=%async_computation.2 | async-start | bytes 524288 | tf_op jit(solution)/shard_map/psum | solution.py:45
  39.9 9.8 %copy-start.2 = (bf16[128,256]{1,0:T(8,128)(2,1)S(1)}, bf16[128,256]{1,0:T(8,128)(2,1)}, u32[]{:S(2)}) copy-start(bf16[128,256]{1,0:T(8,128)(2,1)} %param.20) | copy-start | bytes 196612
  39.9 9.8 %copy-start.3 = (bf16[128,128]{1,0:T(8,128)(2,1)S(1)}, bf16[128,128]{1,0:T(8,128)(2,1)}, u32[]{:S(2)}) copy-start(bf16[128,128]{1,0:T(8,128)(2,1)} %param.12) | copy-start | bytes 98308
  39.9 61.6 %copy-start.8 = (s32[128]{0:T(128)S(1)}, s32[128]{0:T(128)}, u32[]{:S(2)}) copy-start(s32[128]{0:T(128)} %param.19) | copy-start | bytes 1540
  39.9 67.6 %copy-start.5 = (bf16[128,256]{1,0:T(8,128)(2,1)S(1)}, bf16[128,256]{1,0:T(8,128)(2,1)}, u32[]{:S(2)}) copy-start(bf16[128,256]{1,0:T(8,128)(2,1)} %param.21) | copy-start | bytes 196612
  39.9 67.6 %copy-start.7 = (f32[256]{0:T(256)S(1)}, f32[256]{0:T(256)}, u32[]{:S(2)}) copy-start(f32[256]{0:T(256)} %param.22) | copy-start | bytes 3076
  39.9 68.4 %copy-start.6 = (bf16[128,256]{1,0:T(8,128)(2,1)S(1)}, bf16[128,256]{1,0:T(8,128)(2,1)}, u32[]{:S(2)}) copy-start(bf16[128,256]{1,0:T(8,128)(2,1)} %param.23) | copy-start | bytes 196612
  48.9 0.7 copy-start.1
  96.9 10.5 %all-to-all-start = ((f32[8,1,1,16,128]{4,3,1,2,0:T(8,128)}), f32[8,1,1,16,128]{4,3,1,2,0:T(8,128)S(1)}, u32[]{:S(2)}, u32[]{:S(2)}) async-start(f32[8,1,1,16,128]{4,3,1,2,0:T(8,128)} %dynamic-slice_bitcast_fusion), calls=%async_computation | async-start | bytes 131072 | tf_op jit(solution)/shard_map/all_to_all | solution.py:47
  116.7 4.8 %collective-permute-start = (bf16[8,1,1,16,128]{4,3,1,0,2:T(8,128)(2,1)S(1)}, bf16[8,1,1,16,128]{4,3,1,0,2:T(8,128)(2,1)S(1)}, u32[]{:S(2)}, u32[]{:S(2)}) collective-permute-start(bf16[8,1,1,16,128]{4,3,1,0,2:T(8,128)(2,1)S(1)} %bitcast.85), channel_id=1, source_target_pairs={{0,1},{1,2},{2,3},{3,0},{4,5},{5,6},{6,7},{7,4},{8,9},{9,10},{10,1... | collective-permute-start | bytes 98312 | tf_op jit(solution)/shard_map/ppermute | solution.py:67
  121.5 4.8 %collective-permute-start.1 = (bf16[8,1,1,16,128]{4,3,1,0,2:T(8,128)(2,1)S(1)}, bf16[8,1,1,16,128]{4,3,1,0,2:T(8,128)(2,1)S(1)}, u32[]{:S(2)}, u32[]{:S(2)}) collective-permute-start(bf16[8,1,1,16,128]{4,3,1,0,2:T(8,128)(2,1)S(1)} %collective-permute-done), channel_id=1, source_target_pairs={{0,1},{1,2},{2,3},{3,0},{4,5},{5,6},{6,7},{7,4},{8,9},{9,10},{10,1... | collective-permute-start | bytes 98312 | tf_op jit(solution)/shard_map/ppermute | solution.py:67
  126.3 4.8 %collective-permute-start.2 = (bf16[8,1,1,16,128]{4,3,1,0,2:T(8,128)(2,1)S(1)}, bf16[8,1,1,16,128]{4,3,1,0,2:T(8,128)(2,1)S(1)}, u32[]{:S(2)}, u32[]{:S(2)}) collective-permute-start(bf16[8,1,1,16,128]{4,3,1,0,2:T(8,128)(2,1)S(1)} %collective-permute-done.1), channel_id=1, source_target_pairs={{0,1},{1,2},{2,3},{3,0},{4,5},{5,6},{6,7},{7,4},{8,9},{9,10},{10,1... | collective-permute-start | bytes 98312 | tf_op jit(solution)/shard_map/ppermute | solution.py:67
  132.1 4.7 %copy-start.4 = (s32[256]{0:T(256)S(1)}, s32[256]{0:T(256)}, u32[]{:S(2)}) copy-start(s32[256]{0:T(256)} %param.16) | copy-start | bytes 3076
Sparse Core Ops, SparseCore 0:
  49.8 45.6 all-reduce.1
